TPU v7x, 32 devices: a whole 2x2x4 slice. The times are simulated.
32 devices in a mesh: depth: 2 (over y), lat: 8 (over z, x), freq: 2 (over core).
Axes of the slice: x: 2, y: 2, z: 4, core: 2. Of those that a mesh axis runs over, the one named last changes fastest.
Arguments:
- surface: bfloat16 [6, 2, 128, 8192], P('freq', None, None, 'lat'), may hold values from -6 to 6
- refl: float32 [2, 8192], P('depth', 'lat'), may hold values from -0.5 to 0.5
- pool: bfloat16 [2, 6, 8, 128, 256], P('depth', 'freq'), may hold values from -0.375 to 0.375
- tile_ids: int32 [2, 64, 10], P('depth', 'lat'), may hold values from 0 to 63, as said below
- block_ids: int32 [2, 64, 10], P('depth', 'lat'), may hold values from 0 to 7
- counts: int32 [2, 64], P('depth', 'lat'), may hold values from 1 to 10, as said below
Outputs:
- image: float32 [2, 8192], P('depth', 'lat')
Inputs may be any that keep to these rules, and one draw needn't show every extreme that they name: tile_ids[l, j, k] = (j + o) mod 64 for an offset o with -8 <= o <= 8; slot 0 names the row's own tile; in every level some row has all 10 slots live with offsets 8 at slot 1 and -8 at slot 2. Slots k >= counts[l, j] of row j are padding; in every level some row has all 10 slots live.
All inputs are finite; a program needn't handle non-finite values.
Results may differ from a plain program's by a relative error of at most 0.00055.
Values may be sent and summed in bfloat16 or wider, within the bound.
No kernel may reach another device: no remote copies, remote signals or barrier semaphores. Data moves between devices by JAX's collectives and lax.ppermute only.
A program may use at most 128 MiB of HBM per device.

v0:
```python
import jax
import jax.numpy as jnp
from jax import lax
from jax.sharding import PartitionSpec as P

TILE = 128
TILE_DEV = 8


def extended_2(block, sides, width):
    for axis, dim in sides:
        count = lax.axis_size(axis)
        forward = [(i, i + 1) for i in range(count - 1)]
        forward.append((count - 1, 0))
        backward = [(target, source) for source, target in forward]
        low = lax.ppermute(
            lax.slice_in_dim(block, block.shape[dim] - width, None, axis=dim), axis, forward
        )
        high = lax.ppermute(lax.slice_in_dim(block, 0, width, axis=dim), axis, backward)
        block = jnp.concatenate([low, block, high], axis=dim)
    return block


def aperture_rim(wave_field):
    return extended_2(wave_field, (("lat", 3),), TILE_DEV * TILE)


def extrapolate(extended, pool_level, local_ids, block_level, count_level, refl_level):
    freqs_here = extended.shape[0]
    shot_rows = extended.shape[2]
    tile_rows = local_ids.shape[0]
    slot_total = local_ids.shape[1]
    tile_grid = extended.reshape(freqs_here, 2, shot_rows, -1, TILE)
    slot_live = (jnp.arange(slot_total)[None, :] < count_level[:, None]).astype(jnp.bfloat16)
    picked = jnp.take(tile_grid, local_ids, axis=3) * slot_live[None, None, None, :, :, None]
    chosen = jnp.take(pool_level, block_level, axis=1)
    product = jnp.einsum("fsarkt,frktc->rfsac", picked, chosen, preferred_element_type=jnp.float32)
    real_part = product[:, :, 0, :, :TILE] - product[:, :, 1, :, TILE:]
    imag_part = product[:, :, 0, :, TILE:] + product[:, :, 1, :, :TILE]
    row_scale = 1.0 / jnp.sqrt(count_level.astype(jnp.float32))
    rows_out = jnp.stack([real_part, imag_part], 2) * row_scale[:, None, None, None, None]
    wave_out = jnp.transpose(rows_out, (1, 2, 3, 0, 4)).reshape(
        freqs_here, 2, shot_rows, tile_rows * TILE
    )
    wave_out = wave_out * (1.0 - refl_level)
    return (wave_out.astype(jnp.bfloat16), jnp.sum(wave_out * wave_out, axis=(0, 1, 2)))


def per_device(surface, refl, pool, tile_ids, block_ids, counts):
    depth_index = lax.axis_index("depth")
    lat_index = lax.axis_index("lat")
    tile_count = TILE_DEV * lax.axis_size("lat")
    first_tile = lat_index * TILE_DEV - TILE_DEV
    freqs_here = surface.shape[0]
    shot_total = surface.shape[2]
    lateral_width = surface.shape[3]
    shot_rows = shot_total // lax.axis_size("depth")
    own_shots = lax.dynamic_slice_in_dim(surface, depth_index * shot_rows, shot_rows, 2)
    pool_all = lax.all_gather(pool, "depth", axis=0, tiled=True)
    ids_all, blocks_all, counts_all = (
        lax.all_gather(tile_ids, "depth", axis=0, tiled=True),
        lax.all_gather(block_ids, "depth", axis=0, tiled=True),
        lax.all_gather(counts, "depth", axis=0, tiled=True),
    )
    refl_all = lax.all_gather(refl, "depth", axis=0, tiled=True)
    level_total = pool_all.shape[0]

    def level_step(level_index, loop_state):
        wave_field, images = loop_state
        ids_here = lax.dynamic_index_in_dim(ids_all, level_index, 0, keepdims=False)
        local_level = jnp.mod(ids_here - first_tile, tile_count)
        pool_here = lax.dynamic_index_in_dim(pool_all, level_index, 0, keepdims=False)
        blocks_here = lax.dynamic_index_in_dim(blocks_all, level_index, 0, keepdims=False)
        counts_here = lax.dynamic_index_in_dim(counts_all, level_index, 0, keepdims=False)
        refl_here = lax.dynamic_index_in_dim(refl_all, level_index, 0, keepdims=False)
        handed, partial_value = extrapolate(
            aperture_rim(wave_field), pool_here, local_level, blocks_here, counts_here, refl_here
        )
        images = lax.dynamic_update_index_in_dim(images, partial_value, level_index, 0)
        return (handed, images)

    start_images = jnp.zeros((level_total, lateral_width), jnp.float32)
    loop_state = lax.fori_loop(0, level_total, level_step, (own_shots, start_images))
    image_local = lax.psum_scatter(loop_state[1], "depth", scatter_dimension=0, tiled=True)[0]
    summed = lax.psum(image_local, "freq")
    divisor = freqs_here * lax.axis_size("freq") * shot_total
    return (summed / divisor)[None, :]


def solution(mesh):
    placed = (
        P("freq", None, None, "lat"),
        P("depth", "lat"),
        P("depth", "freq", None, None, None),
        P("depth", "lat", None),
        P("depth", "lat", None),
        P("depth", "lat"),
    )
    return jax.shard_map(
        per_device, mesh=mesh, in_specs=placed, out_specs=P("depth", "lat"), check_vma=False
    )
```

profile of v0, /device:TPU:0, one launch (start us, length us, event | category | flops | bytes accessed | tf_op | source)
XLA Modules:
  0.0 194.0 jit_solution(9081155011961694617)
XLA Ops:
  7.3 5.4 %all-gather = s32[2,1,8]{2,1,0:T(1,128)S(1)} all-gather(s32[1,1,8]{2,1,0:T(1,128)} %bitcast.109), channel_id=1, replica_groups=mesh['depth'=2,'lat'=8,'freq'=2] {'depth'}, dimensions={0}, use_global_device_ids=true | all-gather | bytes 96 | tf_op jit(solution)/shard_map/all_gather | solution.py:63
  12.7 4.5 %all-gather.1 = f32[2,1,1024]{2,1,0:T(1,128)S(1)} all-gather(f32[1,1,1024]{2,1,0:T(1,128)} %bitcast.108), channel_id=1, replica_groups=mesh['depth'=2,'lat'=8,'freq'=2] {'depth'}, dimensions={0}, use_global_device_ids=true | all-gather | bytes 12288 | tf_op jit(solution)/shard_map/all_gather | solution.py:65
  17.2 1.2 dynamic-slice
  18.4 4.5 %all_gather.15 = s32[2,8,10]{2,1,0:T(8,128)S(1)} all-gather(s32[1,8,10]{2,1,0:T(8,128)} %param.11), channel_id=1, replica_groups=mesh['depth'=2,'lat'=8,'freq'=2] {'depth'}, dimensions={0}, use_global_device_ids=true | all-gather | bytes 960 | tf_op jit(solution)/shard_map/all_gather | solution.py:61
  22.9 4.8 %all_gather.17 = s32[2,8,10]{2,1,0:T(8,128)S(1)} all-gather(s32[1,8,10]{2,1,0:T(8,128)} %param.12), channel_id=1, replica_groups=mesh['depth'=2,'lat'=8,'freq'=2] {'depth'}, dimensions={0}, use_global_device_ids=true | all-gather | bytes 960 | tf_op jit(solution)/shard_map/all_gather | solution.py:62
  28.7 28.0 %all-gather.4.cloned.1.call-done = bf16[2,3,8,128,256]{4,3,2,1,0:T(8,128)(2,1)} async-done(((bf16[1,3,8,128,256]{4,3,2,1,0:T(8,128)(2,1)}), bf16[2,3,8,128,256]{4,3,2,1,0:T(8,128)(2,1)}) %all-gather.4.cloned.1.call-update) | async-done | bytes 3145744 | tf_op jit(solution)/shard_map/all_gather | solution.py:59
  56.7 121.8 %while.17 = (s32[]{:T(128)}, bf16[3,2,64,1024]{3,2,1,0:T(8,128)(2,1)}, f32[2,1024]{1,0:T(2,128)S(1)}, s32[2,8,10]{2,1,0:T(8,128)S(1)}, s32[]{:T(128)}, /*index=5...) while((s32[]{:T(128)}, ...), condition=%wide.region_2.3_spmd, body=%wide.region_0.2_spmd.sunk | while | flops 2040010240 | bytes 96773536 | solution.py:83
  56.7 4.2 %collective-permute-start = (bf16[3,2,64,1024]{3,2,1,0:T(8,128)(2,1)}, bf16[3,2,64,1024]{3,2,1,0:T(8,128)(2,1)}, u32[]{:S(2)}, u32[]{:S(2)}) collective-permute-start(bf16[3,2,64,1024]{3,2,1,0:T(8,128)(2,1)} %get-tuple-element.336), channel_id=1, source_target_pairs={{2,0},{4,2},{6,4},{8,6},{10,8},{12,10},{14,12},{0,14},{3,1},{5,3},... | collective-permute-start | bytes 2359304 | tf_op jit(solution)/shard_map/while/body/eval_jaxpr/ppermute | solution.py:19
  60.9 1.5 dynamic-slice_bitcast_fusion.2
  62.6 8.2 %gather_fusion = bf16[80,3,128,256]{3,2,1,0:T(8,128)(2,1)} fusion(bf16[3,8,128,256]{3,2,1,0:T(8,128)(2,1)S(1)} %dynamic-slice_bitcast_fusion.2, s32[1024]{0:T(1024)S(1)} %pad_clamp_fusion.4), kind=kCustom, calls=%fused_computation.1.clone.1 | custom fusion | bytes 31457600 | tf_op jit(solution)/shard_map/while/body/eval_jaxpr/jit(_take)/gather | solution.py:36
  71.0 22.1 %collective-permute-done = bf16[3,2,64,1024]{3,2,1,0:T(8,128)(2,1)} collective-permute-done((bf16[3,2,64,1024]{3,2,1,0:T(8,128)(2,1)}, bf16[3,2,64,1024]{3,2,1,0:T(8,128)(2,1)}, u32[]{:S(2)}, u32[]{:S(2)}) %collective-permute-start) | collective-permute-done | bytes 786464 | tf_op jit(solution)/shard_map/while/body/eval_jaxpr/ppermute | solution.py:19
  93.1 3.6 %copy_bitcast_fusion.3 = bf16[3,2,64,24,128]{4,2,3,1,0:T(8,128)(2,1)} fusion(bf16[3,2,64,1024]{3,2,1,0:T(8,128)(2,1)} %collective-permute-done, bf16[3,2,64,1024]{3,2,1,0:T(8,128)(2,1)} %get-tuple-element.336, bf16[3,2,64,1024]{3,2,1,0:T(8,128)(2,1)} %collective-permute-done.1), kind=kLoop, calls=%fused_computation.7.clone.1 | loop fusion | flops 7077888 | bytes 4718592 | tf_op jit(solution)/shard_map/while/body/eval_jaxpr/reshape | solution.py:33
  96.7 8.5 %gather_fusion.1 = bf16[80,3,2,64,128]{4,3,2,1,0:T(8,128)(2,1)} fusion(bf16[3,2,64,24,128]{4,2,3,1,0:T(8,128)(2,1)} %copy_bitcast_fusion.3, s32[1024]{0:T(1024)S(1)} %pad_clamp_fusion.5), kind=kCustom, calls=%fused_computation.clone.1 | custom fusion | bytes 15728960 | tf_op jit(solution)/shard_map/while/body/eval_jaxpr/jit(_take)/gather | solution.py:35
  105.2 10.2 %fusion.29 = f32[8,3,2,64,256]{4,3,2,1,0:T(8,128)S(1)} fusion(bf16[8,10,3,128,256]{4,3,2,1,0:T(8,128)(2,1)} %bitcast.101, pred[8,10]{1,0:T(8,128)(4,1)S(1)} %get-tuple-element.317, bf16[8,10,3,2,64,128]{5,4,3,2,1,0:T(8,128)(2,1)} %bitcast.100, pred[8,10]{1,0:T(8,128)(4,1)S(1)} %get-tuple-element.319, bf16[8,10]{1,0:T(8,128)(2,1)S(1)} %fusion.28), kind=kOutput, calls=%fused_computation.9.clone.1 | convolution fusion | flops 2028994560 | bytes 26739008 | tf_op jit(solution)/shard_map/while/body/eval_jaxpr/fsarkt,frktc->rfsac/dot_general | solution.py:37
  117.2 4.5 %collective-permute-start = (bf16[3,2,64,1024]{3,2,1,0:T(8,128)(2,1)}, bf16[3,2,64,1024]{3,2,1,0:T(8,128)(2,1)}, u32[]{:S(2)}, u32[]{:S(2)}) collective-permute-start(bf16[3,2,64,1024]{3,2,1,0:T(8,128)(2,1)} %get-tuple-element.336), channel_id=1, source_target_pairs={{2,0},{4,2},{6,4},{8,6},{10,8},{12,10},{14,12},{0,14},{3,1},{5,3},... | collective-permute-start | bytes 2359304 | tf_op jit(solution)/shard_map/while/body/eval_jaxpr/ppermute | solution.py:19
  121.7 1.5 dynamic-slice_bitcast_fusion.2
  123.4 8.2 %gather_fusion = bf16[80,3,128,256]{3,2,1,0:T(8,128)(2,1)} fusion(bf16[3,8,128,256]{3,2,1,0:T(8,128)(2,1)S(1)} %dynamic-slice_bitcast_fusion.2, s32[1024]{0:T(1024)S(1)} %pad_clamp_fusion.4), kind=kCustom, calls=%fused_computation.1.clone.1 | custom fusion | bytes 31457600 | tf_op jit(solution)/shard_map/while/body/eval_jaxpr/jit(_take)/gather | solution.py:36
  131.7 22.7 %collective-permute-done = bf16[3,2,64,1024]{3,2,1,0:T(8,128)(2,1)} collective-permute-done((bf16[3,2,64,1024]{3,2,1,0:T(8,128)(2,1)}, bf16[3,2,64,1024]{3,2,1,0:T(8,128)(2,1)}, u32[]{:S(2)}, u32[]{:S(2)}) %collective-permute-start) | collective-permute-done | bytes 786464 | tf_op jit(solution)/shard_map/while/body/eval_jaxpr/ppermute | solution.py:19
  154.4 3.6 %copy_bitcast_fusion.3 = bf16[3,2,64,24,128]{4,2,3,1,0:T(8,128)(2,1)} fusion(bf16[3,2,64,1024]{3,2,1,0:T(8,128)(2,1)} %collective-permute-done, bf16[3,2,64,1024]{3,2,1,0:T(8,128)(2,1)} %get-tuple-element.336, bf16[3,2,64,1024]{3,2,1,0:T(8,128)(2,1)} %collective-permute-done.1), kind=kLoop, calls=%fused_computation.7.clone.1 | loop fusion | flops 7077888 | bytes 4718592 | tf_op jit(solution)/shard_map/while/body/eval_jaxpr/reshape | solution.py:33
  158.0 8.5 %gather_fusion.1 = bf16[80,3,2,64,128]{4,3,2,1,0:T(8,128)(2,1)} fusion(bf16[3,2,64,24,128]{4,2,3,1,0:T(8,128)(2,1)} %copy_bitcast_fusion.3, s32[1024]{0:T(1024)S(1)} %pad_clamp_fusion.5), kind=kCustom, calls=%fused_computation.clone.1 | custom fusion | bytes 15728960 | tf_op jit(solution)/shard_map/while/body/eval_jaxpr/jit(_take)/gather | solution.py:35
  166.6 10.2 %fusion.29 = f32[8,3,2,64,256]{4,3,2,1,0:T(8,128)S(1)} fusion(bf16[8,10,3,128,256]{4,3,2,1,0:T(8,128)(2,1)} %bitcast.101, pred[8,10]{1,0:T(8,128)(4,1)S(1)} %get-tuple-element.317, bf16[8,10,3,2,64,128]{5,4,3,2,1,0:T(8,128)(2,1)} %bitcast.100, pred[8,10]{1,0:T(8,128)(4,1)S(1)} %get-tuple-element.319, bf16[8,10]{1,0:T(8,128)(2,1)S(1)} %fusion.28), kind=kOutput, calls=%fused_computation.9.clone.1 | convolution fusion | flops 2028994560 | bytes 26739008 | tf_op jit(solution)/shard_map/while/body/eval_jaxpr/fsarkt,frktc->rfsac/dot_general | solution.py:37
  177.3 1.2 fusion.30
  178.5 5.0 %all-reduce = f32[2,1024]{1,0:T(2,128)S(1)} all-reduce(f32[2,1024]{1,0:T(2,128)S(1)} %get-tuple-element.226), channel_id=2, replica_groups=mesh['depth'=2,'lat'=8,'freq'=2] {'depth'}, use_global_device_ids=true, to_apply=%region_3.4.clone | all-reduce | flops 2048 | bytes 16384
  184.1 2.5 %psum.7 = f32[1024]{0:T(1024)S(1)} all-reduce(f32[1024]{0:T(1024)S(1)} %bitcast.106), channel_id=1, replica_groups=mesh['depth'=2,'lat'=8,'freq'=2] {'freq'}, use_global_device_ids=true, to_apply=%region_4.5 | all-reduce | flops 1024 | bytes 8192 | tf_op jit(solution)/shard_map/psum | solution.py:85
  (38 shorter events, 5.7 us)
Async XLA Ops:
  6.5 21.1 %copy-start = (bf16[3,2,128,1024]{3,2,1,0:T(8,128)(2,1)S(1)}, bf16[3,2,128,1024]{3,2,1,0:T(8,128)(2,1)}, u32[]{:S(2)}) copy-start(bf16[3,2,128,1024]{3,2,1,0:T(8,128)(2,1)} %param.8) | copy-start | bytes 4718596
  6.5 50.1 %all-gather.4.cloned.1.call-start = ((), (), s32[]{:S(2)}) async-start(), calls=%async_computation | async-start | bytes 4718592 | tf_op jit(solution)/shard_map/all_gather | solution.py:59
  56.7 36.4 %collective-permute-start = (bf16[3,2,64,1024]{3,2,1,0:T(8,128)(2,1)}, bf16[3,2,64,1024]{3,2,1,0:T(8,128)(2,1)}, u32[]{:S(2)}, u32[]{:S(2)}) collective-permute-start(bf16[3,2,64,1024]{3,2,1,0:T(8,128)(2,1)} %get-tuple-element.336), channel_id=1, source_target_pairs={{2,0},{4,2},{6,4},{8,6},{10,8},{12,10},{14,12},{0,14},{3,1},{5,3},... | collective-permute-start | bytes 2359304 | tf_op jit(solution)/shard_map/while/body/eval_jaxpr/ppermute | solution.py:19
  60.9 32.1 %collective-permute-start.1 = (bf16[3,2,64,1024]{3,2,1,0:T(8,128)(2,1)}, bf16[3,2,64,1024]{3,2,1,0:T(8,128)(2,1)}, u32[]{:S(2)}, u32[]{:S(2)}) collective-permute-start(bf16[3,2,64,1024]{3,2,1,0:T(8,128)(2,1)} %get-tuple-element.336), channel_id=1, source_target_pairs={{0,2},{2,4},{4,6},{6,8},{8,10},{10,12},{12,14},{14,0},{1,3},{3,5},... | collective-permute-start | bytes 2359304 | tf_op jit(solution)/shard_map/while/body/eval_jaxpr/ppermute | solution.py:16
  117.2 37.2 %collective-permute-start = (bf16[3,2,64,1024]{3,2,1,0:T(8,128)(2,1)}, bf16[3,2,64,1024]{3,2,1,0:T(8,128)(2,1)}, u32[]{:S(2)}, u32[]{:S(2)}) collective-permute-start(bf16[3,2,64,1024]{3,2,1,0:T(8,128)(2,1)} %get-tuple-element.336), channel_id=1, source_target_pairs={{2,0},{4,2},{6,4},{8,6},{10,8},{12,10},{14,12},{0,14},{3,1},{5,3},... | collective-permute-start | bytes 2359304 | tf_op jit(solution)/shard_map/while/body/eval_jaxpr/ppermute | solution.py:19
  121.7 32.8 %collective-permute-start.1 = (bf16[3,2,64,1024]{3,2,1,0:T(8,128)(2,1)}, bf16[3,2,64,1024]{3,2,1,0:T(8,128)(2,1)}, u32[]{:S(2)}, u32[]{:S(2)}) collective-permute-start(bf16[3,2,64,1024]{3,2,1,0:T(8,128)(2,1)} %get-tuple-element.336), channel_id=1, source_target_pairs={{0,2},{2,4},{4,6},{6,8},{8,10},{10,12},{12,14},{14,0},{1,3},{3,5},... | collective-permute-start | bytes 2359304 | tf_op jit(solution)/shard_map/while/body/eval_jaxpr/ppermute | solution.py:16
Sparse Core Ops, SparseCore 0:
  8.9 47.7 all-gather.3
where the time goes:
time: 194 us
  waiting for transfers between devices  73.5 us (38%)
  local copies, waits for them, and re-layouts  39.6 us (20%)
  blocking collectives  26.7 us (14%)
  matrix products  20.5 us (11%)
  between operations  13.4 us (7%)
  other arithmetic  11.5 us (6%)
  starting transfers between devices  8.71 us (4%)
    ppermute x2, waiting for transfers between devices, extended_2(): lax.ppermute(lax.slice_in_dim(block, 0, width, axis=dim), axis, backward)  44.8 us
    all_gather x1, waiting for transfers between devices, per_device(): pool_all = lax.all_gather(pool, 'depth', axis=0, tiled=True)  28 us
    dot_general x2, matrix products, extrapolate(): jnp.einsum('fsarkt,frktc->rfsac', picked, chosen, preferred_element_type=...  20.5 us
    gather x2, local copies, waits for them, and re-layouts, extrapolate(): jnp.take(tile_grid, local_ids, axis=3)  17 us
    gather x2, local copies, waits for them, and re-layouts, extrapolate(): chosen = jnp.take(pool_level, block_level, axis=1)  16.4 us
    ppermute x2, starting transfers between devices, extended_2(): lax.ppermute(lax.slice_in_dim(block, 0, width, axis=dim), axis, backward)  8.71 us
    reshape x2, other arithmetic, extrapolate(): tile_grid = extended.reshape(freqs_here, 2, shot_rows, -1, TILE)  7.29 us
    all_gather x1, blocking collectives, per_device(): lax.all_gather(counts, 'depth', axis=0, tiled=True)  5.4 us
  transfers between devices with their start and end apart: 5, of which 3 were waited for; matrix products, arithmetic and copies ran while one was open for 11% of the time, Pallas kernels for 0%

commit v1 on v0

--- a/solution.py
+++ b/solution.py
@@ -5,6 +5,24 @@
 
 TILE = 128
 TILE_DEV = 8
+
+
+def laid_out(blocks, dim):
+    shape = list(blocks.shape[1:])
+    shape[dim] *= blocks.shape[0]
+    return jnp.moveaxis(blocks, 0, dim).reshape(shape)
+
+
+def doubled(array, axis):
+    devices = lax.axis_size(axis)
+    blocks = array[None]
+    for level in range(devices.bit_length() - 1):
+        bit = 1 << level
+        received = lax.ppermute(blocks, axis, [(i, i ^ bit) for i in range(devices)])
+        both = jnp.stack([blocks, received])
+        upper = lax.axis_index(axis) >> level & 1
+        blocks = jnp.where(upper == 0, both, both[::-1]).reshape(-1, *array.shape)
+    return blocks
 
 
 def extended_2(block, sides, width):
@@ -56,7 +74,7 @@
     lateral_width = surface.shape[3]
     shot_rows = shot_total // lax.axis_size("depth")
     own_shots = lax.dynamic_slice_in_dim(surface, depth_index * shot_rows, shot_rows, 2)
-    pool_all = lax.all_gather(pool, "depth", axis=0, tiled=True)
+    pool_all = laid_out(doubled(pool, "depth"), 0)
     ids_all, blocks_all, counts_all = (
         lax.all_gather(tile_ids, "depth", axis=0, tiled=True),
         lax.all_gather(block_ids, "depth", axis=0, tiled=True),

time: 194 us -> 185 us (0.954)
  waiting for transfers between devices: 73.5 us -> 40 us
  blocking collectives: 26.7 us -> 55.6 us
  between operations: 13.4 us -> 0.03 us
  other arithmetic: 11.5 us -> 15.7 us
  starting transfers between devices: 8.71 us -> 12.5 us
    all_gather x1, blocking collectives: 5.4 us -> 34.7 us  [per_device(): lax.all_gather(counts, 'depth', axis=0, tiled=True)]
    all_gather x1 -> x0, waiting for transfers between devices: 28 us -> none  [per_device(): pool_all = lax.all_gather(pool, 'depth', axis=0, tiled=True)]
    ppermute x2, waiting for transfers between devices: 44.8 us -> 40 us  [extended_2(): lax.ppermute(lax.slice_in_dim(block, 0, width, axis=dim), axis, backward)]
    another operation x0 -> x2, other arithmetic: none -> 4.25 us  [the longest x1 2.56 us: laid_out(): return jnp.moveaxis(blocks, 0, dim).reshape(shape)]
    ppermute x0 -> x1, starting transfers between devices: none -> 3 us  [doubled(): lax.ppermute(blocks, axis, [(i, i ^ bit) for i in range(devices)])]
  transfers between devices with their start and end apart: 5 -> 5, of which waited for: 3 -> 2; matrix products, arithmetic and copies ran while one was open for 11% -> 12% of each run, Pallas kernels for 0% -> 0%
where the time goes in v1:
time: 185 us; the launch traced here: 184 us
  blocking collectives  55.6 us (30%)
  waiting for transfers between devices  40 us (22%)
  local copies, waits for them, and re-layouts  39.7 us (21%)
  matrix products  20.5 us (11%)
  other arithmetic  15.7 us (8%)
  starting transfers between devices  12.5 us (7%)
    ppermute x2, waiting for transfers between devices, extended_2(): lax.ppermute(lax.slice_in_dim(block, 0, width, axis=dim), axis, backward)  40 us
    all_gather x1, blocking collectives, per_device(): lax.all_gather(counts, 'depth', axis=0, tiled=True)  34.7 us
    dot_general x2, matrix products, extrapolate(): jnp.einsum('fsarkt,frktc->rfsac', picked, chosen, preferred_element_type=...  20.5 us
    gather x2, local copies, waits for them, and re-layouts, extrapolate(): jnp.take(tile_grid, local_ids, axis=3)  17 us
    gather x2, local copies, waits for them, and re-layouts, extrapolate(): chosen = jnp.take(pool_level, block_level, axis=1)  16.4 us
    ppermute x2, starting transfers between devices, extended_2(): lax.ppermute(lax.slice_in_dim(block, 0, width, axis=dim), axis, backward)  9.53 us
    reshape x2, other arithmetic, extrapolate(): tile_grid = extended.reshape(freqs_here, 2, shot_rows, -1, TILE)  7.31 us
    unnamed x1, blocking collectives  5 us
  transfers between devices with their start and end apart: 5, of which 2 were waited for; matrix products, arithmetic and copies ran while one was open for 12% of the time, Pallas kernels for 0%

profile of v1, /device:TPU:0, one launch (start us, length us, event | category | flops | bytes accessed | tf_op | source)
XLA Modules:
  0.0 184.3 jit_solution(8825564734286021359)
XLA Ops:
  0.0 3.0 %collective-permute-start.2 = (bf16[1,1,3,8,128,256]{5,4,3,2,1,0:T(8,128)(2,1)}, bf16[1,1,3,8,128,256]{5,4,3,2,1,0:T(8,128)(2,1)S(1)}, u32[]{:S(2)}, u32[]{:S(2)}) collective-permute-start(bf16[1,1,3,8,128,256]{5,4,3,2,1,0:T(8,128)(2,1)} %bitcast.107), channel_id=1, source_target_pairs={{0,16},{16,0},{1,17},{17,1},{2,18},{18,2},{3,19},{19,3},{4,20},{20... | collective-permute-start | bytes 4718600 | tf_op jit(solution)/shard_map/ppermute | solution.py:21
  3.0 34.7 %all-gather = s32[2,1,8]{2,1,0:T(1,128)S(1)} all-gather(s32[1,1,8]{2,1,0:T(1,128)} %bitcast.117), channel_id=1, replica_groups=mesh['depth'=2,'lat'=8,'freq'=2] {'depth'}, dimensions={0}, use_global_device_ids=true | all-gather | bytes 96 | tf_op jit(solution)/shard_map/all_gather | solution.py:81
  37.7 4.5 %all-gather.1 = f32[2,1,1024]{2,1,0:T(1,128)S(1)} all-gather(f32[1,1,1024]{2,1,0:T(1,128)} %bitcast.116), channel_id=1, replica_groups=mesh['depth'=2,'lat'=8,'freq'=2] {'depth'}, dimensions={0}, use_global_device_ids=true | all-gather | bytes 12288 | tf_op jit(solution)/shard_map/all_gather | solution.py:83
  43.5 4.5 %all_gather.12 = s32[2,8,10]{2,1,0:T(8,128)S(1)} all-gather(s32[1,8,10]{2,1,0:T(8,128)} %param.11), channel_id=1, replica_groups=mesh['depth'=2,'lat'=8,'freq'=2] {'depth'}, dimensions={0}, use_global_device_ids=true | all-gather | bytes 960 | tf_op jit(solution)/shard_map/all_gather | solution.py:79
  48.0 4.5 %all_gather.14 = s32[2,8,10]{2,1,0:T(8,128)S(1)} all-gather(s32[1,8,10]{2,1,0:T(8,128)} %param.12), channel_id=1, replica_groups=mesh['depth'=2,'lat'=8,'freq'=2] {'depth'}, dimensions={0}, use_global_device_ids=true | all-gather | bytes 960 | tf_op jit(solution)/shard_map/all_gather | solution.py:80
  53.5 1.7 pad_maximum_fusion
  55.2 2.6 %fusion.16 = bf16[2,3,8,128,256]{4,3,2,1,0:T(8,128)(2,1)} fusion(bf16[2,1,1,3,8,128,256]{6,5,4,3,0,2,1:T(8,128)(2,1)S(1)} %pad_maximum_fusion, pred[]{:T(512)S(6)} %eq.11), kind=kLoop, calls=%fused_computation.44 | loop fusion | flops 1572864 | bytes 6291457 | tf_op jit(solution)/shard_map/reshape;reshape | solution.py:13
  57.7 117.8 %while.17 = (s32[]{:T(128)}, bf16[3,2,64,1024]{3,2,1,0:T(8,128)(2,1)}, f32[2,1024]{1,0:T(2,128)S(1)}, s32[2,8,10]{2,1,0:T(8,128)S(1)}, s32[]{:T(128)}, /*index=5...) while((s32[]{:T(128)}, ...), condition=%wide.region_2.3_spmd, body=%wide.region_0.2_spmd.sunk | while | flops 2040010240 | bytes 96773536 | solution.py:101
  57.7 4.8 %collective-permute-start = (bf16[3,2,64,1024]{3,2,1,0:T(8,128)(2,1)}, bf16[3,2,64,1024]{3,2,1,0:T(8,128)(2,1)}, u32[]{:S(2)}, u32[]{:S(2)}) collective-permute-start(bf16[3,2,64,1024]{3,2,1,0:T(8,128)(2,1)} %get-tuple-element.336), channel_id=1, source_target_pairs={{2,0},{4,2},{6,4},{8,6},{10,8},{12,10},{14,12},{0,14},{3,1},{5,3},... | collective-permute-start | bytes 2359304 | tf_op jit(solution)/shard_map/while/body/eval_jaxpr/ppermute | solution.py:37
  62.5 1.5 dynamic-slice_bitcast_fusion.2
  64.2 8.2 %gather_fusion = bf16[80,3,128,256]{3,2,1,0:T(8,128)(2,1)} fusion(bf16[3,8,128,256]{3,2,1,0:T(8,128)(2,1)S(1)} %dynamic-slice_bitcast_fusion.2, s32[1024]{0:T(1024)S(1)} %pad_clamp_fusion.4), kind=kCustom, calls=%fused_computation.1.clone.1 | custom fusion | bytes 31457600 | tf_op jit(solution)/shard_map/while/body/eval_jaxpr/jit(_take)/gather | solution.py:54
  72.5 17.5 %collective-permute-done = bf16[3,2,64,1024]{3,2,1,0:T(8,128)(2,1)} collective-permute-done((bf16[3,2,64,1024]{3,2,1,0:T(8,128)(2,1)}, bf16[3,2,64,1024]{3,2,1,0:T(8,128)(2,1)}, u32[]{:S(2)}, u32[]{:S(2)}) %collective-permute-start) | collective-permute-done | bytes 786464 | tf_op jit(solution)/shard_map/while/body/eval_jaxpr/ppermute | solution.py:37
  90.0 3.7 %copy_bitcast_fusion.3 = bf16[3,2,64,24,128]{4,2,3,1,0:T(8,128)(2,1)} fusion(bf16[3,2,64,1024]{3,2,1,0:T(8,128)(2,1)} %collective-permute-done, bf16[3,2,64,1024]{3,2,1,0:T(8,128)(2,1)} %get-tuple-element.336, bf16[3,2,64,1024]{3,2,1,0:T(8,128)(2,1)} %collective-permute-done.1), kind=kLoop, calls=%fused_computation.7.clone.1 | loop fusion | flops 7077888 | bytes 4718592 | tf_op jit(solution)/shard_map/while/body/eval_jaxpr/reshape | solution.py:51
  93.7 8.5 %gather_fusion.1 = bf16[80,3,2,64,128]{4,3,2,1,0:T(8,128)(2,1)} fusion(bf16[3,2,64,24,128]{4,2,3,1,0:T(8,128)(2,1)} %copy_bitcast_fusion.3, s32[1024]{0:T(1024)S(1)} %pad_clamp_fusion.5), kind=kCustom, calls=%fused_computation.clone.1 | custom fusion | bytes 15728960 | tf_op jit(solution)/shard_map/while/body/eval_jaxpr/jit(_take)/gather | solution.py:53
  102.2 10.2 %fusion.30 = f32[8,3,2,64,256]{4,3,2,1,0:T(8,128)S(1)} fusion(bf16[8,10,3,128,256]{4,3,2,1,0:T(8,128)(2,1)} %bitcast.106, pred[8,10]{1,0:T(8,128)(4,1)S(1)} %get-tuple-element.317, bf16[8,10,3,2,64,128]{5,4,3,2,1,0:T(8,128)(2,1)} %bitcast.105, pred[8,10]{1,0:T(8,128)(4,1)S(1)} %get-tuple-element.319, bf16[8,10]{1,0:T(8,128)(2,1)S(1)} %fusion.29), kind=kOutput, calls=%fused_computation.9.clone.1 | convolution fusion | flops 2028994560 | bytes 26739008 | tf_op jit(solution)/shard_map/while/body/eval_jaxpr/fsarkt,frktc->rfsac/dot_general | solution.py:55
  114.2 4.8 %collective-permute-start = (bf16[3,2,64,1024]{3,2,1,0:T(8,128)(2,1)}, bf16[3,2,64,1024]{3,2,1,0:T(8,128)(2,1)}, u32[]{:S(2)}, u32[]{:S(2)}) collective-permute-start(bf16[3,2,64,1024]{3,2,1,0:T(8,128)(2,1)} %get-tuple-element.336), channel_id=1, source_target_pairs={{2,0},{4,2},{6,4},{8,6},{10,8},{12,10},{14,12},{0,14},{3,1},{5,3},... | collective-permute-start | bytes 2359304 | tf_op jit(solution)/shard_map/while/body/eval_jaxpr/ppermute | solution.py:37
  118.9 1.5 dynamic-slice_bitcast_fusion.2
  120.7 8.2 %gather_fusion = bf16[80,3,128,256]{3,2,1,0:T(8,128)(2,1)} fusion(bf16[3,8,128,256]{3,2,1,0:T(8,128)(2,1)S(1)} %dynamic-slice_bitcast_fusion.2, s32[1024]{0:T(1024)S(1)} %pad_clamp_fusion.4), kind=kCustom, calls=%fused_computation.1.clone.1 | custom fusion | bytes 31457600 | tf_op jit(solution)/shard_map/while/body/eval_jaxpr/jit(_take)/gather | solution.py:54
  129.0 22.5 %collective-permute-done = bf16[3,2,64,1024]{3,2,1,0:T(8,128)(2,1)} collective-permute-done((bf16[3,2,64,1024]{3,2,1,0:T(8,128)(2,1)}, bf16[3,2,64,1024]{3,2,1,0:T(8,128)(2,1)}, u32[]{:S(2)}, u32[]{:S(2)}) %collective-permute-start) | collective-permute-done | bytes 786464 | tf_op jit(solution)/shard_map/while/body/eval_jaxpr/ppermute | solution.py:37
  151.4 3.7 %copy_bitcast_fusion.3 = bf16[3,2,64,24,128]{4,2,3,1,0:T(8,128)(2,1)} fusion(bf16[3,2,64,1024]{3,2,1,0:T(8,128)(2,1)} %collective-permute-done, bf16[3,2,64,1024]{3,2,1,0:T(8,128)(2,1)} %get-tuple-element.336, bf16[3,2,64,1024]{3,2,1,0:T(8,128)(2,1)} %collective-permute-done.1), kind=kLoop, calls=%fused_computation.7.clone.1 | loop fusion | flops 7077888 | bytes 4718592 | tf_op jit(solution)/shard_map/while/body/eval_jaxpr/reshape | solution.py:51
  155.1 8.5 %gather_fusion.1 = bf16[80,3,2,64,128]{4,3,2,1,0:T(8,128)(2,1)} fusion(bf16[3,2,64,24,128]{4,2,3,1,0:T(8,128)(2,1)} %copy_bitcast_fusion.3, s32[1024]{0:T(1024)S(1)} %pad_clamp_fusion.5), kind=kCustom, calls=%fused_computation.clone.1 | custom fusion | bytes 15728960 | tf_op jit(solution)/shard_map/while/body/eval_jaxpr/jit(_take)/gather | solution.py:53
  163.6 10.2 %fusion.30 = f32[8,3,2,64,256]{4,3,2,1,0:T(8,128)S(1)} fusion(bf16[8,10,3,128,256]{4,3,2,1,0:T(8,128)(2,1)} %bitcast.106, pred[8,10]{1,0:T(8,128)(4,1)S(1)} %get-tuple-element.317, bf16[8,10,3,2,64,128]{5,4,3,2,1,0:T(8,128)(2,1)} %bitcast.105, pred[8,10]{1,0:T(8,128)(4,1)S(1)} %get-tuple-element.319, bf16[8,10]{1,0:T(8,128)(2,1)S(1)} %fusion.29), kind=kOutput, calls=%fused_computation.9.clone.1 | convolution fusion | flops 2028994560 | bytes 26739008 | tf_op jit(solution)/shard_map/while/body/eval_jaxpr/fsarkt,frktc->rfsac/dot_general | solution.py:55
  175.6 5.0 %all-reduce = f32[2,1024]{1,0:T(2,128)S(1)} all-reduce(f32[2,1024]{1,0:T(2,128)S(1)} %get-tuple-element.226), channel_id=2, replica_groups=mesh['depth'=2,'lat'=8,'freq'=2] {'depth'}, use_global_device_ids=true, to_apply=%region_3.4.clone | all-reduce | flops 2048 | bytes 16384
  181.2 2.5 %psum.7 = f32[1024]{0:T(1024)S(1)} all-reduce(f32[1024]{0:T(1024)S(1)} %bitcast.114), channel_id=1, replica_groups=mesh['depth'=2,'lat'=8,'freq'=2] {'freq'}, use_global_device_ids=true, to_apply=%region_4.5 | all-reduce | flops 1024 | bytes 8192 | tf_op jit(solution)/shard_map/psum | solution.py:103
  (39 shorter events, 7.5 us)
Async XLA Ops:
  0.0 52.5 %copy-start = (bf16[3,2,128,1024]{3,2,1,0:T(8,128)(2,1)S(1)}, bf16[3,2,128,1024]{3,2,1,0:T(8,128)(2,1)}, u32[]{:S(2)}) copy-start(bf16[3,2,128,1024]{3,2,1,0:T(8,128)(2,1)} %param.8) | copy-start | bytes 4718596
  0.0 53.5 %collective-permute-start.2 = (bf16[1,1,3,8,128,256]{5,4,3,2,1,0:T(8,128)(2,1)}, bf16[1,1,3,8,128,256]{5,4,3,2,1,0:T(8,128)(2,1)S(1)}, u32[]{:S(2)}, u32[]{:S(2)}) collective-permute-start(bf16[1,1,3,8,128,256]{5,4,3,2,1,0:T(8,128)(2,1)} %bitcast.107), channel_id=1, source_target_pairs={{0,16},{16,0},{1,17},{17,1},{2,18},{18,2},{3,19},{19,3},{4,20},{20... | collective-permute-start | bytes 4718600 | tf_op jit(solution)/shard_map/ppermute | solution.py:21
  57.7 32.3 %collective-permute-start = (bf16[3,2,64,1024]{3,2,1,0:T(8,128)(2,1)}, bf16[3,2,64,1024]{3,2,1,0:T(8,128)(2,1)}, u32[]{:S(2)}, u32[]{:S(2)}) collective-permute-start(bf16[3,2,64,1024]{3,2,1,0:T(8,128)(2,1)} %get-tuple-element.336), channel_id=1, source_target_pairs={{2,0},{4,2},{6,4},{8,6},{10,8},{12,10},{14,12},{0,14},{3,1},{5,3},... | collective-permute-start | bytes 2359304 | tf_op jit(solution)/shard_map/while/body/eval_jaxpr/ppermute | solution.py:37
  62.5 27.6 %collective-permute-start.1 = (bf16[3,2,64,1024]{3,2,1,0:T(8,128)(2,1)}, bf16[3,2,64,1024]{3,2,1,0:T(8,128)(2,1)}, u32[]{:S(2)}, u32[]{:S(2)}) collective-permute-start(bf16[3,2,64,1024]{3,2,1,0:T(8,128)(2,1)} %get-tuple-element.336), channel_id=1, source_target_pairs={{0,2},{2,4},{4,6},{6,8},{8,10},{10,12},{12,14},{14,0},{1,3},{3,5},... | collective-permute-start | bytes 2359304 | tf_op jit(solution)/shard_map/while/body/eval_jaxpr/ppermute | solution.py:34
  114.2 37.3 %collective-permute-start = (bf16[3,2,64,1024]{3,2,1,0:T(8,128)(2,1)}, bf16[3,2,64,1024]{3,2,1,0:T(8,128)(2,1)}, u32[]{:S(2)}, u32[]{:S(2)}) collective-permute-start(bf16[3,2,64,1024]{3,2,1,0:T(8,128)(2,1)} %get-tuple-element.336), channel_id=1, source_target_pairs={{2,0},{4,2},{6,4},{8,6},{10,8},{12,10},{14,12},{0,14},{3,1},{5,3},... | collective-permute-start | bytes 2359304 | tf_op jit(solution)/shard_map/while/body/eval_jaxpr/ppermute | solution.py:37
  118.9 32.5 %collective-permute-start.1 = (bf16[3,2,64,1024]{3,2,1,0:T(8,128)(2,1)}, bf16[3,2,64,1024]{3,2,1,0:T(8,128)(2,1)}, u32[]{:S(2)}, u32[]{:S(2)}) collective-permute-start(bf16[3,2,64,1024]{3,2,1,0:T(8,128)(2,1)} %get-tuple-element.336), channel_id=1, source_target_pairs={{0,2},{2,4},{4,6},{6,8},{8,10},{10,12},{12,14},{14,0},{1,3},{3,5},... | collective-permute-start | bytes 2359304 | tf_op jit(solution)/shard_map/while/body/eval_jaxpr/ppermute | solution.py:34
